TPU v7x, 256 devices: a whole 4x4x8 slice. The times are simulated.
256 devices in a mesh: dp: 8 (over z), expert: 32 (over x, y, core).
Axes of the slice: x: 4, y: 4, z: 8, core: 2. Of those that a mesh axis runs over, the one named last changes fastest.
Arguments:
- tokens: bfloat16 [256, 212, 1024], P(('dp', 'expert')), may hold values from -6 to 6
- expert_ids: int32 [256, 212, 1], P(('dp', 'expert')), may hold values from 0 to 31; in each aligned block of 212 rows (0 to 211, 212 to 423, ..., all dimensions but the last counted through in order) at most 9 rows name the same one
- caption_lengths: int32 [256], P(('dp', 'expert')), may hold values from 1 to 16, as said below
- layer_norm_gain: float32 [1024], replicated, may hold values from 0.5 to 1.5
- router: float32 [1024, 32], replicated, may hold values from -0.1875 to 0.1875
- w_up: bfloat16 [32, 1024, 4096], P('expert', None, 'dp'), may hold values from -0.1875 to 0.1875
- w_down: bfloat16 [32, 4096, 1024], P('expert', 'dp'), may hold values from -0.09375 to 0.09375
- logit_scale: float32 [1], replicated, may hold values from 5 to 20
- logit_bias: float32 [1], replicated, may hold values from -4 to -1.5
Outputs:
- loss: float32 [1], replicated
- grad_tokens: bfloat16 [256, 212, 1024], P(('dp', 'expert'))
- grad_up: float32 [32, 1024, 4096], P('expert', None, 'dp')
- grad_down: float32 [32, 4096, 1024], P('expert', 'dp')
- grad_router: float32 [1024, 32], replicated
- layer_gain_gradient: float32 [1024], replicated
Inputs may be any that keep to these rules, and one draw needn't show every extreme that they name: `expert_ids`: among the rows of one device (aligned blocks of 212 rows, devices ordered by dp then expert) no expert is named more than 9 times, a bound that some block reaches. `caption_lengths`: some caption has all 16 tokens.
All inputs are finite; a program needn't handle non-finite values.
Results may differ from a plain program's by a relative error of at most 0.009.
Values may be sent and summed in bfloat16 or wider, within the bound.
No kernel may reach another device: no remote copies, remote signals or barrier semaphores. Data moves between devices by JAX's collectives and lax.ppermute only.
A program may use at most 128 MiB of HBM per device.

v0:
```python
import jax
import jax.numpy as jnp
from jax import lax
from jax.sharding import PartitionSpec as P

D = 1024
PATCH = 196
CAPLEN = 16
SEQ = 212
eps = 1e-06
loss_scale = 1024.0


def gelu_slope(pre):
    return (
        0.5 * (1.0 + lax.erf(pre * 0.7071067811865476))
        + pre * jnp.exp(-0.5 * pre * pre) * 0.3989422804014327
    )


def deliver(buffer, experts, slots):
    width = buffer.shape[-1]
    sent = lax.all_to_all(
        buffer.reshape(experts, 1, slots, width), "expert", split_axis=0, concat_axis=1, tiled=True
    )
    shaped = sent.reshape(sent.shape[0], 1, sent.shape[1], slots, width)
    whole = lax.all_gather(shaped, "dp", axis=1, tiled=True)
    return whole.reshape(whole.shape[0], -1, width)


def give_back(partial_value, n_dp, n_expert, slots):
    local = partial_value.shape[0]
    width = partial_value.shape[-1]
    summed = lax.psum_scatter(
        partial_value.reshape(local, n_dp, n_expert * slots, width).astype(jnp.bfloat16),
        "dp",
        scatter_dimension=1,
        tiled=True,
    )
    rounded = summed.reshape(local, n_expert, slots, width)
    returned = lax.all_to_all(rounded, "expert", split_axis=1, concat_axis=0, tiled=True)
    return returned.reshape(-1, width)


def body(
    tokens,
    expert_ids,
    caption_lengths,
    layer_norm_gain,
    router,
    w_up,
    w_down,
    logit_scale,
    logit_bias,
):
    n_dp = lax.axis_size("dp")
    n_expert = lax.axis_size("expert")
    pair_dev = tokens.shape[0]
    rows = pair_dev * SEQ
    experts = router.shape[1]
    slots = rows * 4 // (3 * experts) + 1
    pairs_all = pair_dev * n_dp * n_expert
    input_rows = tokens.reshape(rows, D).astype(jnp.float32)
    input_mean = jnp.mean(input_rows, axis=1, keepdims=True)
    var_x = jnp.mean((input_rows - input_mean) ** 2, axis=1, keepdims=True)
    inverse_deviation = 1.0 / jnp.sqrt(var_x + eps)
    centered_scaled_input = (input_rows - input_mean) * inverse_deviation
    normalized_input = (centered_scaled_input * layer_norm_gain).astype(jnp.bfloat16)
    ids = expert_ids.reshape(rows)
    onehot = (ids[:, None] == jnp.arange(experts, dtype=jnp.int32)[None, :]).astype(jnp.int32)
    slot = jnp.sum((jnp.cumsum(onehot, axis=0) - 1) * onehot, axis=1)
    dest = ids * slots + slot
    onehot_f = onehot.astype(jnp.float32)
    buffer = jnp.zeros((experts * slots, D), jnp.bfloat16).at[dest].set(normalized_input)
    gathered = deliver(buffer, experts, slots)
    pre = jnp.einsum("erd,edf->erf", gathered, w_up, preferred_element_type=jnp.float32)
    act = jax.nn.gelu(pre, approximate=False).astype(jnp.bfloat16)
    partial_value = jnp.einsum("erf,efd->erd", act, w_down, preferred_element_type=jnp.float32)
    moe = give_back(partial_value, n_dp, n_expert, slots)[dest].astype(jnp.float32)
    xnf = normalized_input.astype(jnp.float32)
    router_logits = jnp.dot(xnf, router, precision=lax.Precision.HIGHEST)
    gate = jax.nn.sigmoid(jnp.sum(router_logits * onehot_f, axis=1))
    y = (input_rows + gate[:, None] * moe).reshape(pair_dev, SEQ, D)
    img = jnp.mean(y[:, :PATCH], axis=1)
    lengths = caption_lengths.astype(jnp.float32)
    mask = (jnp.arange(CAPLEN, dtype=jnp.int32)[None, :] < caption_lengths[:, None]).astype(
        jnp.float32
    )
    txt = jnp.sum(y[:, PATCH:] * mask[:, :, None], axis=1) / lengths[:, None]
    ru = jnp.sqrt(jnp.mean(img * img, axis=1, keepdims=True) + eps)
    rv = jnp.sqrt(jnp.mean(txt * txt, axis=1, keepdims=True) + eps)
    u = img / ru
    v = txt / rv
    scale = logit_scale[0]
    first = lax.axis_index(("dp", "expert")) * pair_dev
    mine = first + jnp.arange(pair_dev, dtype=jnp.int32)
    every = jnp.arange(pairs_all, dtype=jnp.int32)
    own_sign = jnp.where(mine[:, None] == every[None, :], 1.0, -1.0)
    v_all = lax.all_gather(v, ("dp", "expert"), axis=0, tiled=True)
    logits = scale * jnp.dot(u, v_all.T, precision=lax.Precision.HIGHEST) / D + logit_bias[0]
    loss_term = -jnp.sum(jax.nn.log_sigmoid(own_sign * logits)) / pairs_all
    coef = -(loss_scale / pairs_all) * own_sign * jax.nn.sigmoid(-own_sign * logits)
    du = scale / D * jnp.dot(coef, v_all, precision=lax.Precision.HIGHEST)
    dv_terms = scale / D * jnp.dot(coef.T, u, precision=lax.Precision.HIGHEST)
    dv = lax.psum_scatter(dv_terms, ("dp", "expert"), scatter_dimension=0, tiled=True)
    dimg = (du - u * jnp.mean(du * u, axis=1, keepdims=True)) / ru
    dtxt = (dv - v * jnp.mean(dv * v, axis=1, keepdims=True)) / rv
    dy_img = jnp.broadcast_to(dimg[:, None, :] / PATCH, (pair_dev, PATCH, D))
    dy_txt = (dtxt / lengths[:, None])[:, None, :] * mask[:, :, None]
    dy = jnp.concatenate([dy_img, dy_txt], axis=1).reshape(rows, D)
    dmoe = (gate[:, None] * dy).astype(jnp.bfloat16)
    dgl = jnp.sum(dy * moe, axis=1) * gate * (1.0 - gate)
    router_part = jnp.dot(xnf.T, onehot_f * dgl[:, None], precision=lax.Precision.HIGHEST)
    grad_buffer = jnp.zeros((experts * slots, D), jnp.bfloat16).at[dest].set(dmoe)
    gathered_grads = deliver(grad_buffer, experts, slots)
    dact = jnp.einsum("erd,efd->erf", gathered_grads, w_down, preferred_element_type=jnp.float32)
    dpre = (dact * gelu_slope(pre)).astype(jnp.bfloat16)
    grad_down = jnp.einsum("erf,erd->efd", act, gathered_grads, preferred_element_type=jnp.float32)
    grad_up = jnp.einsum("erd,erf->edf", gathered, dpre, preferred_element_type=jnp.float32)
    back_partial = jnp.einsum("erf,edf->erd", dpre, w_up, preferred_element_type=jnp.float32)
    dxe = give_back(back_partial, n_dp, n_expert, slots)[dest].astype(jnp.float32)
    router_rows = jnp.dot(onehot_f, router.T, precision=lax.Precision.HIGHEST)
    gradient_normalized_input = dxe + dgl[:, None] * router_rows
    gain_partial_term = jnp.sum(gradient_normalized_input * centered_scaled_input, axis=0)
    scaled_output_gradient = gradient_normalized_input * layer_norm_gain
    normed_input_gradient = (
        scaled_output_gradient
        - jnp.mean(scaled_output_gradient, axis=1, keepdims=True)
        - centered_scaled_input
        * jnp.mean(scaled_output_gradient * centered_scaled_input, axis=1, keepdims=True)
    ) * inverse_deviation
    grad_tokens = (dy + normed_input_gradient).astype(jnp.bfloat16).reshape(pair_dev, SEQ, D)
    loss, grad_router, layer_gain_gradient = lax.psum(
        (loss_term, router_part, gain_partial_term), ("dp", "expert")
    )
    return (loss.reshape(1), grad_tokens, grad_up, grad_down, grad_router, layer_gain_gradient)


def solution(mesh):
    return jax.shard_map(
        body,
        mesh=mesh,
        in_specs=(
            P(("dp", "expert"), None, None),
            P(("dp", "expert"), None, None),
            P(("dp", "expert")),
            P(),
            P(),
            P("expert", None, "dp"),
            P("expert", "dp", None),
            P(),
            P(),
        ),
        out_specs=(
            P(),
            P(("dp", "expert"), None, None),
            P("expert", None, "dp"),
            P("expert", "dp", None),
            P(),
            P(),
        ),
        check_vma=False,
    )
```

profile of v0, /device:TPU:8, one launch (start us, length us, event | category | flops | bytes accessed | tf_op | source)
XLA Modules:
  0.0 1022.8 jit_solution(2046483523152713916)
XLA Ops:
  12.8 2.3 scatter_custom_fusion
  15.4 22.9 %all_to_all.16 = bf16[32,1,9,1024]{3,2,1,0:T(8,128)(2,1)S(1)} all-to-all(bf16[32,1,9,1024]{3,2,1,0:T(8,128)(2,1)S(1)} %bitcast.149), channel_id=1, replica_groups=mesh['dp'=8,'expert'=32] {'expert'}, dimensions={0} | all-to-all | bytes 1179648 | tf_op jit(solution)/shard_map/all_to_all | solution.py:23
  39.7 60.3 %all-gather.7.cloned.1.call-done = bf16[256,1,9,1024]{3,0,2,1:T(8,128)(2,1)} async-done(((bf16[32,1,9,1024]{3,0,2,1:T(8,128)(2,1)}), bf16[256,1,9,1024]{3,0,2,1:T(8,128)(2,1)}) %all-gather.7.cloned.1.call-update) | async-done | bytes 4718608 | tf_op jit(solution)/shard_map/all_gather | solution.py:27
  100.0 8.7 copy.22
  108.7 9.8 reshape.491
  118.6 14.9 %fusion.2 = (bf16[2304,512]{1,0:T(8,128)(2,1)S(1)}, f32[2304,512]{1,0:T(8,128)}) fusion(bf16[2304,1024]{1,0:T(8,128)(2,1)} %reshape.491, bf16[1,1024,512]{2,1,0:T(8,128)(2,1)S(1)} %copy-done), kind=kOutput, calls=%fused_computation.9 | convolution fusion | flops 2492596224 | bytes 12845056 | tf_op jit(solution)/shard_map/erd,edf->erf/dot_general | solution.py:76
  134.8 4.2 convert_bitcast_fusion.1
  139.8 58.3 %reduce-scatter.3.cloned.1.call-done = bf16[1,1,288,1024]{3,2,1,0:T(8,128)(2,1)} async-done(((bf16[1,8,288,1024]{3,2,1,0:T(8,128)(2,1)}), bf16[1,1,288,1024]{3,2,1,0:T(8,128)(2,1)}) %reduce-scatter.3.cloned.1.call-update) | async-done | bytes 589840 | tf_op jit(solution)/shard_map/reduce_scatter | solution.py:34
  198.1 2.2 reshape.494
  200.2 7.4 all-to-all-start.1
  208.8 14.4 %all-to-all-done.1 = bf16[1,32,9,1024]{3,2,0,1:T(8,128)(2,1)S(1)} async-done(((bf16[1,32,9,1024]{3,2,0,1:T(8,128)(2,1)}), bf16[1,32,9,1024]{3,2,0,1:T(8,128)(2,1)S(1)}, u32[]{:S(2)}, u32[]{:S(2)}) %all-to-all-start.1) | async-done | bytes 589856 | tf_op jit(solution)/shard_map/all_to_all | solution.py:41
  229.8 95.7 %all-gather.9.cloned.1.call-done = f32[262144]{0:T(1024)} async-done(((f32[1024]{0:T(1024)}), f32[262144]{0:T(1024)}) %all-gather.9.cloned.1.call-update) | async-done | bytes 1048592 | tf_op jit(solution)/shard_map/all_gather | solution.py:99
  331.5 254.7 %all-reduce.8.cloned.1.call-done = f32[256,1024]{1,0:T(8,128)} async-done(((f32[256,1024]{1,0:T(8,128)}), f32[256,1024]{1,0:T(8,128)}) %all-reduce.8.cloned.1.call-update) | async-done | bytes 1048592
  589.2 2.5 scatter_custom_fusion.1
  593.0 22.3 %all_to_all.17 = bf16[32,1,9,1024]{3,2,1,0:T(8,128)(2,1)S(1)} all-to-all(bf16[32,1,9,1024]{3,2,1,0:T(8,128)(2,1)S(1)} %bitcast.150), channel_id=1, replica_groups=mesh['dp'=8,'expert'=32] {'expert'}, dimensions={0} | all-to-all | bytes 1179648 | tf_op jit(solution)/shard_map/all_to_all | solution.py:23
  616.6 57.0 %all-gather.11.cloned.1.call-done = bf16[256,1,9,1024]{3,0,2,1:T(8,128)(2,1)} async-done(((bf16[32,1,9,1024]{3,0,2,1:T(8,128)(2,1)}), bf16[256,1,9,1024]{3,0,2,1:T(8,128)(2,1)}) %all-gather.11.cloned.1.call-update) | async-done | bytes 4718608 | tf_op jit(solution)/shard_map/all_gather | solution.py:27
  673.6 8.7 copy.26
  682.3 9.9 reshape.500
  692.2 7.0 fusion.14
  700.6 4.4 convert_bitcast_fusion
  707.3 7.0 convolution_bitcast_fusion
  714.3 49.8 %reduce-scatter.5.cloned.1.call-done = bf16[1,1,288,1024]{3,2,1,0:T(8,128)(2,1)} async-done(((bf16[1,8,288,1024]{3,2,1,0:T(8,128)(2,1)}), bf16[1,1,288,1024]{3,2,1,0:T(8,128)(2,1)}) %reduce-scatter.5.cloned.1.call-update) | async-done | bytes 589840 | tf_op jit(solution)/shard_map/reduce_scatter | solution.py:34
  764.1 2.2 reshape.501
  766.3 7.5 all-to-all-start.3
  773.7 7.1 convolution_bitcast_fusion.1
  780.8 8.6 all-to-all-done.3
  789.4 1.4 reshape.502
  790.8 2.0 gather_fusion.1
  792.8 2.3 fusion.37
  796.3 75.8 %all-reduce.2 = (f32[1]{0:T(128)}, f32[1024]{0:T(1024)}) all-reduce(f32[1]{0:T(128)} %bitcast.20, f32[1024]{0:T(1024)S(1)} %get-tuple-element.6), channel_id=1, replica_groups=mesh['dp'=8,'expert'=32] {'dp','expert'}, use_global_device_ids=true, to_apply=%region_13.14 | all-reduce | flops 1025 | bytes 8200 | tf_op jit(solution)/shard_map/psum | solution.py:133
  872.1 142.3 %all-reduce.6.cloned.1.call-done = f32[1024,32]{0,1:T(8,128)} async-done(((f32[1024,32]{0,1:T(8,128)}), f32[1024,32]{0,1:T(8,128)}) %all-reduce.6.cloned.1.call-update) | async-done | bytes 131088 | tf_op jit(solution)/shard_map/psum | solution.py:133
  1014.4 1.6 copy.37
  (117 shorter events, 27.8 us)
Async XLA Ops:
  7.2 111.4 %copy-start = (bf16[1,1024,512]{2,1,0:T(8,128)(2,1)S(1)}, bf16[1,1024,512]{2,1,0:T(8,128)(2,1)}, u32[]{:S(2)}) copy-start(bf16[1,1024,512]{2,1,0:T(8,128)(2,1)} %param.14) | copy-start | bytes 3145732
  7.2 92.8 %all-gather.7.cloned.1.call-start = ((), (), s32[]{:S(2)}) async-start(), calls=%async_computation.9 | async-start | bytes 5308416 | tf_op jit(solution)/shard_map/all_gather | solution.py:27
  8.5 199.2 %copy-start.11 = (f32[212]{0:T(256)}, f32[212]{0:T(256)S(1)}, u32[]{:S(2)}) copy-start(f32[212]{0:T(256)S(1)} %broadcast_multiply_fusion.3) | copy-start | bytes 2548
  9.8 197.9 %copy-start.15 = (f32[212]{0:T(256)}, f32[212]{0:T(256)S(1)}, u32[]{:S(2)}) copy-start(f32[212]{0:T(256)S(1)} %add_rsqrt_fusion) | copy-start | bytes 2548
  12.8 127.0 %copy-start.22 = (s32[212,1]{0,1:T(1,128)}, s32[212,1]{0,1:T(1,128)S(1)}, u32[]{:S(2)}) copy-start(s32[212,1]{0,1:T(1,128)S(1)} %compare_select_fusion) | copy-start | bytes 2548
  39.4 158.6 %reduce-scatter.3.cloned.1.call-start = ((), (), s32[]{:S(2)}) async-start(), calls=%async_computation.6 | async-start | bytes 5308416 | tf_op jit(solution)/shard_map/reduce_scatter | solution.py:34
  118.6 16.3 %copy-start.25 = (bf16[1,512,1024]{2,1,0:T(8,128)(2,1)S(1)}, bf16[1,512,1024]{2,1,0:T(8,128)(2,1)}, u32[]{:S(2)}) copy-start(bf16[1,512,1024]{2,1,0:T(8,128)(2,1)} %param.15) | copy-start | bytes 3145732
  133.4 1.4 copy-start.27
  139.0 68.7 %copy-start.1 = (bf16[1,212,1024]{2,1,0:T(8,128)(2,1)S(1)}, bf16[1,212,1024]{2,1,0:T(8,128)(2,1)}, u32[]{:S(2)}) copy-start(bf16[1,212,1024]{2,1,0:T(8,128)(2,1)} %param.9) | copy-start | bytes 1302532
  139.0 68.7 %copy-start.9 = (f32[1024]{0:T(1024)S(1)}, f32[1024]{0:T(1024)}, u32[]{:S(2)}) copy-start(f32[1024]{0:T(1024)} %param.12) | copy-start | bytes 12292
  139.0 69.0 %copy-start.7 = (f32[1024,32]{0,1:T(8,128)S(1)}, f32[1024,32]{0,1:T(8,128)}, u32[]{:S(2)}) copy-start(f32[1024,32]{0,1:T(8,128)} %param.13) | copy-start | bytes 393220
  139.0 69.0 %copy-start.13 = (s32[1,212,1]{1,2,0:T(1,128)S(1)}, s32[1,212,1]{1,2,0:T(1,128)}, u32[]{:S(2)}) copy-start(s32[1,212,1]{1,2,0:T(1,128)} %param.10) | copy-start | bytes 2548
  139.8 85.0 %copy-start.23 = (f32[16]{0:T(128)}, f32[16]{0:T(128)S(1)}, u32[]{:S(2)}) copy-start(f32[16]{0:T(128)S(1)} %compare_convert_fusion) | copy-start | bytes 196
  139.8 83.7 %copy-start.17 = (s32[1024]{0:T(1024)}, s32[1024]{0:T(1024)S(1)}, u32[]{:S(2)}) copy-start(s32[1024]{0:T(1024)S(1)} %pad_clamp_fusion) | copy-start | bytes 12292
  200.2 23.0 %all-to-all-start.1 = ((bf16[1,32,9,1024]{3,2,0,1:T(8,128)(2,1)}), bf16[1,32,9,1024]{3,2,0,1:T(8,128)(2,1)S(1)}, u32[]{:S(2)}, u32[]{:S(2)}) async-start(bf16[1,32,9,1024]{3,2,0,1:T(8,128)(2,1)} %bitcast.148), calls=%async_computation.2 | async-start | bytes 2097152 | tf_op jit(solution)/shard_map/all_to_all | solution.py:41
  207.7 117.8 %all-gather.9.cloned.1.call-start = ((), (), s32[]{:S(2)}) async-start(), calls=%async_computation.10 | async-start | bytes 1052672 | tf_op jit(solution)/shard_map/all_gather | solution.py:99
  208.8 14.7 %copy-start.18 = (f32[212]{0:T(256)}, f32[212]{0:T(256)S(1)}, u32[]{:S(2)}) copy-start(f32[212]{0:T(256)S(1)} %fusion.16) | copy-start | bytes 2548
  208.8 15.8 %copy-start.20 = (f32[212]{0:T(256)}, f32[212]{0:T(256)S(1)}, u32[]{:S(2)}) copy-start(f32[212]{0:T(256)S(1)} %add_divide_fusion) | copy-start | bytes 2548
  224.6 5.2 copy-start.2
  226.8 359.4 %copy-start.8 = (f32[1024]{0:T(1024)S(1)}, f32[1024]{0:T(1024)}, u32[]{:S(2)}) copy-start(f32[1024]{0:T(1024)} %broadcast_divide_fusion) | copy-start | bytes 12292
  226.8 359.4 %all-reduce.8.cloned.1.call-start = ((), (), s32[]{:S(2)}) async-start(), calls=%async_computation.12 | async-start | bytes 2097152
  228.4 360.6 %copy-start.24 = (f32[16]{0:T(128)S(1)}, f32[16]{0:T(128)}, u32[]{:S(2)}) copy-start(f32[16]{0:T(128)} %copy-done.23) | copy-start | bytes 196
  228.4 360.7 %copy-start.21 = (f32[212]{0:T(256)S(1)}, f32[212]{0:T(256)}, u32[]{:S(2)}) copy-start(f32[212]{0:T(256)} %copy-done.20) | copy-start | bytes 2548
  329.6 344.0 %all-gather.11.cloned.1.call-start = ((), (), s32[]{:S(2)}) async-start(), calls=%async_computation.11 | async-start | bytes 5308416 | tf_op jit(solution)/shard_map/all_gather | solution.py:27
  616.5 147.6 %reduce-scatter.5.cloned.1.call-start = ((), (), s32[]{:S(2)}) async-start(), calls=%async_computation.7 | async-start | bytes 5308416 | tf_op jit(solution)/shard_map/reduce_scatter | solution.py:34
  682.3 9.9 copy-start.26
  699.2 1.4 copy-start.6
  705.1 309.3 %all-reduce.6.cloned.1.call-start = ((), (), s32[]{:S(2)}) async-start(), calls=%async_computation.8 | async-start | bytes 262144 | tf_op jit(solution)/shard_map/psum | solution.py:133
  766.3 23.1 %all-to-all-start.3 = ((bf16[1,32,9,1024]{3,2,0,1:T(8,128)(2,1)}), bf16[1,32,9,1024]{3,2,0,1:T(8,128)(2,1)}, u32[]{:S(2)}, u32[]{:S(2)}) async-start(bf16[1,32,9,1024]{3,2,0,1:T(8,128)(2,1)} %bitcast.30), calls=%async_computation.5 | async-start | bytes 2097152 | tf_op jit(solution)/shard_map/all_to_all | solution.py:41
  780.8 12.0 %copy-start.10 = (f32[1024]{0:T(1024)S(1)}, f32[1024]{0:T(1024)}, u32[]{:S(2)}) copy-start(f32[1024]{0:T(1024)} %param.12) | copy-start | bytes 12292
  780.8 12.0 %copy-start.12 = (f32[212]{0:T(256)S(1)}, f32[212]{0:T(256)}, u32[]{:S(2)}) copy-start(f32[212]{0:T(256)} %copy-done.11) | copy-start | bytes 2548
  780.8 12.0 %copy-start.16 = (f32[212]{0:T(256)S(1)}, f32[212]{0:T(256)}, u32[]{:S(2)}) copy-start(f32[212]{0:T(256)} %copy-done.15) | copy-start | bytes 2548
  (5 other events, 5.5 us)
Sparse Core Ops, SparseCore 0:
  39.6 60.3 all-gather.6
  139.2 58.8 reduce-scatter.2
  226.9 98.4 all-gather.8
  331.3 254.8 all-reduce.7
  616.6 56.8 all-gather.10
  705.2 58.8 reduce-scatter.4
  771.1 243.2 all-reduce.5
where the time goes:
time: 1020 us
  waiting for transfers between devices  741 us (73%)
  blocking collectives  121 us (12%)
  local copies, waits for them, and re-layouts  56.6 us (6%)
  matrix products  49.8 us (5%)
  between operations  19.9 us (2%)
  other arithmetic  18.6 us (2%)
  starting transfers between devices  15.8 us (2%)
    unnamed x8, waiting for transfers between devices  255 us
    psum x1, waiting for transfers between devices, body(): lax.psum((loss_term, router_part, gain_partial_term), ('dp', 'expert'))  142 us
    all_gather x2, waiting for transfers between devices, deliver(): whole = lax.all_gather(shaped, 'dp', axis=1, tiled=True)  117 us
    reduce_scatter x2, waiting for transfers between devices, give_back(): lax.psum_scatter(partial_value.reshape(local, n_dp, n_expert * slots, wid...  108 us
    all_gather x1, waiting for transfers between devices, body(): v_all = lax.all_gather(v, ('dp', 'expert'), axis=0, tiled=True)  95.7 us
    psum x1, blocking collectives, body(): lax.psum((loss_term, router_part, gain_partial_term), ('dp', 'expert'))  75.8 us
    all_to_all x2, blocking collectives, deliver(): lax.all_to_all(buffer.reshape(experts, 1, slots, width), 'expert', split_...  45.2 us
    all_to_all x2, waiting for transfers between devices, give_back(): lax.all_to_all(rounded, 'expert', split_axis=1, concat_axis=0, tiled=True)  23 us
  transfers between devices with their start and end apart: 9, of which 9 were waited for; matrix products, arithmetic and copies ran while one was open for 3% of the time, Pallas kernels for 0%

commit v1 on v0

--- a/solution.py
+++ b/solution.py
@@ -1,3 +1,4 @@
+import functools
 import jax
 import jax.numpy as jnp
 from jax import lax
@@ -9,6 +10,15 @@
 SEQ = 212
 eps = 1e-06
 loss_scale = 1024.0
+
+
+def scan_spots(local_array, along_axis, axis_key):
+    for ix in (along_axis, axis_key):
+        local_array = lax.psum(local_array, ix)
+    return local_array
+
+
+raise_teams_for = functools.partial(scan_spots, along_axis="dp", axis_key="expert")
 
 
 def gelu_slope(pre):
@@ -130,8 +140,8 @@
         * jnp.mean(scaled_output_gradient * centered_scaled_input, axis=1, keepdims=True)
     ) * inverse_deviation
     grad_tokens = (dy + normed_input_gradient).astype(jnp.bfloat16).reshape(pair_dev, SEQ, D)
-    loss, grad_router, layer_gain_gradient = lax.psum(
-        (loss_term, router_part, gain_partial_term), ("dp", "expert")
+    loss, grad_router, layer_gain_gradient = raise_teams_for(
+        (loss_term, router_part, gain_partial_term)
     )
     return (loss.reshape(1), grad_tokens, grad_up, grad_down, grad_router, layer_gain_gradient)
 

time: 1020 us -> 933 us (0.915)
  waiting for transfers between devices: 741 us -> 645 us
    psum x1 -> x2, waiting for transfers between devices: 142 us -> 45.4 us  [scan_spots(): local_array = lax.psum(local_array, ix)]
    psum x1 -> x2, blocking collectives: 75.8 us -> 76.6 us  [scan_spots(): local_array = lax.psum(local_array, ix)]
    unnamed x8 -> x9, waiting for transfers between devices: 255 us -> 255 us
  transfers between devices with their start and end apart: 9 -> 10, of which waited for: 9 -> 10; matrix products, arithmetic and copies ran while one was open for 3% -> 6% of each run, Pallas kernels for 0% -> 0%
where the time goes in v1:
time: 933 us; the launch traced here: 930 us
  waiting for transfers between devices  645 us (69%)
  blocking collectives  122 us (13%)
  local copies, waits for them, and re-layouts  56.5 us (6%)
  matrix products  50.7 us (5%)
  other arithmetic  20.2 us (2%)
  between operations  19.8 us (2%)
  starting transfers between devices  15.9 us (2%)
    unnamed x9, waiting for transfers between devices  255 us
    all_gather x2, waiting for transfers between devices, deliver(): whole = lax.all_gather(shaped, 'dp', axis=1, tiled=True)  113 us
    reduce_scatter x2, waiting for transfers between devices, give_back(): lax.psum_scatter(partial_value.reshape(local, n_dp, n_expert * slots, wid...  113 us
    all_gather x1, waiting for transfers between devices, body(): v_all = lax.all_gather(v, ('dp', 'expert'), axis=0, tiled=True)  95.7 us
    psum x2, blocking collectives, scan_spots(): local_array = lax.psum(local_array, ix)  76.6 us
    psum x2, waiting for transfers between devices, scan_spots(): local_array = lax.psum(local_array, ix)  45.4 us
    all_to_all x2, blocking collectives, deliver(): lax.all_to_all(buffer.reshape(experts, 1, slots, width), 'expert', split_...  45.2 us
    all_to_all x2, waiting for transfers between devices, give_back(): lax.all_to_all(rounded, 'expert', split_axis=1, concat_axis=0, tiled=True)  23.1 us
  transfers between devices with their start and end apart: 10, of which 10 were waited for; matrix products, arithmetic and copies ran while one was open for 6% of the time, Pallas kernels for 0%

profile of v1, /device:TPU:8, one launch (start us, length us, event | category | flops | bytes accessed | tf_op | source)
XLA Modules:
  0.0 929.7 jit_solution(6629440776206208300)
XLA Ops:
  12.8 2.3 scatter_custom_fusion
  15.4 22.9 %all_to_all.16 = bf16[32,1,9,1024]{3,2,1,0:T(8,128)(2,1)S(1)} all-to-all(bf16[32,1,9,1024]{3,2,1,0:T(8,128)(2,1)S(1)} %bitcast.149), channel_id=1, replica_groups=mesh['dp'=8,'expert'=32] {'expert'}, dimensions={0} | all-to-all | bytes 1179648 | tf_op jit(solution)/shard_map/all_to_all | solution.py:33
  39.7 60.3 %all-gather.7.cloned.1.call-done = bf16[256,1,9,1024]{3,0,2,1:T(8,128)(2,1)} async-done(((bf16[32,1,9,1024]{3,0,2,1:T(8,128)(2,1)}), bf16[256,1,9,1024]{3,0,2,1:T(8,128)(2,1)}) %all-gather.7.cloned.1.call-update) | async-done | bytes 4718608 | tf_op jit(solution)/shard_map/all_gather | solution.py:37
  100.0 8.7 copy.22
  108.7 9.8 %reshape.491 = bf16[2304,1024]{1,0:T(8,128)(2,1)} reshape(bf16[256,1,9,1024]{3,2,0,1:T(8,128)(2,1)} %copy.22) | data formatting | bytes 9437184 | tf_op jit(solution)/shard_map/reshape.7
  118.6 14.9 %fusion.2 = (bf16[2304,512]{1,0:T(8,128)(2,1)S(1)}, f32[2304,512]{1,0:T(8,128)}) fusion(bf16[2304,1024]{1,0:T(8,128)(2,1)} %reshape.491, bf16[1,1024,512]{2,1,0:T(8,128)(2,1)S(1)} %copy-done), kind=kOutput, calls=%fused_computation.9 | convolution fusion | flops 2492596224 | bytes 12845056 | tf_op jit(solution)/shard_map/erd,edf->erf/dot_general | solution.py:86
  134.8 4.2 convert_bitcast_fusion.1
  139.8 58.3 %reduce-scatter.3.cloned.1.call-done = bf16[1,1,288,1024]{3,2,1,0:T(8,128)(2,1)} async-done(((bf16[1,8,288,1024]{3,2,1,0:T(8,128)(2,1)}), bf16[1,1,288,1024]{3,2,1,0:T(8,128)(2,1)}) %reduce-scatter.3.cloned.1.call-update) | async-done | bytes 589840 | tf_op jit(solution)/shard_map/reduce_scatter | solution.py:44
  198.1 2.2 reshape.494
  200.2 7.4 all-to-all-start.1
  208.8 14.4 %all-to-all-done.1 = bf16[1,32,9,1024]{3,2,0,1:T(8,128)(2,1)S(1)} async-done(((bf16[1,32,9,1024]{3,2,0,1:T(8,128)(2,1)}), bf16[1,32,9,1024]{3,2,0,1:T(8,128)(2,1)S(1)}, u32[]{:S(2)}, u32[]{:S(2)}) %all-to-all-start.1) | async-done | bytes 589856 | tf_op jit(solution)/shard_map/all_to_all | solution.py:51
  229.8 95.7 %all-gather.9.cloned.1.call-done = f32[262144]{0:T(1024)} async-done(((f32[1024]{0:T(1024)}), f32[262144]{0:T(1024)}) %all-gather.9.cloned.1.call-update) | async-done | bytes 1048592 | tf_op jit(solution)/shard_map/all_gather | solution.py:109
  331.5 254.7 %all-reduce.12.cloned.1.call-done = f32[256,1024]{1,0:T(8,128)} async-done(((f32[256,1024]{1,0:T(8,128)}), f32[256,1024]{1,0:T(8,128)}) %all-reduce.12.cloned.1.call-update) | async-done | bytes 1048592
  589.2 2.5 scatter_custom_fusion.1
  593.0 22.3 %all_to_all.17 = bf16[32,1,9,1024]{3,2,1,0:T(8,128)(2,1)S(1)} all-to-all(bf16[32,1,9,1024]{3,2,1,0:T(8,128)(2,1)S(1)} %bitcast.150), channel_id=1, replica_groups=mesh['dp'=8,'expert'=32] {'expert'}, dimensions={0} | all-to-all | bytes 1179648 | tf_op jit(solution)/shard_map/all_to_all | solution.py:33
  618.5 2.0 fusion.51
  620.5 53.0 %all-gather.11.cloned.1.call-done = bf16[256,1,9,1024]{3,0,2,1:T(8,128)(2,1)} async-done(((bf16[32,1,9,1024]{3,0,2,1:T(8,128)(2,1)}), bf16[256,1,9,1024]{3,0,2,1:T(8,128)(2,1)}) %all-gather.11.cloned.1.call-update) | async-done | bytes 4718608 | tf_op jit(solution)/shard_map/all_gather | solution.py:37
  673.6 8.7 copy.26
  682.3 9.9 %reshape.500 = bf16[2304,1024]{1,0:T(8,128)(2,1)} reshape(bf16[256,1,9,1024]{3,2,0,1:T(8,128)(2,1)} %copy.26) | data formatting | bytes 9437184 | tf_op jit(solution)/shard_map/reshape.64
  692.2 6.8 fusion.14
  700.4 4.4 convert_bitcast_fusion
  705.7 41.2 %all-reduce.8.cloned.1.call-done = f32[1024,32]{0,1:T(8,128)} async-done(((f32[1024,32]{0,1:T(8,128)}), f32[1024,32]{0,1:T(8,128)}) %all-reduce.8.cloned.1.call-update) | async-done | bytes 131088 | tf_op jit(solution)/shard_map/psum | solution.py:17
  747.0 7.0 convolution_bitcast_fusion
  753.9 54.3 %reduce-scatter.5.cloned.1.call-done = bf16[1,1,288,1024]{3,2,1,0:T(8,128)(2,1)} async-done(((bf16[1,8,288,1024]{3,2,1,0:T(8,128)(2,1)}), bf16[1,1,288,1024]{3,2,1,0:T(8,128)(2,1)}) %reduce-scatter.5.cloned.1.call-update) | async-done | bytes 589840 | tf_op jit(solution)/shard_map/reduce_scatter | solution.py:44
  808.2 2.2 reshape.501
  810.4 7.5 all-to-all-start.3
  817.9 7.1 convolution_bitcast_fusion.1
  824.9 8.6 all-to-all-done.3
  837.0 2.3 fusion.37
  840.5 16.2 %all-reduce.3 = (f32[]{:T(128)}, f32[1024]{0:T(1024)S(1)}) all-reduce(f32[]{:T(128)S(6)} %div.153, f32[1024]{0:T(1024)S(1)} %get-tuple-element.6), channel_id=1, replica_groups=mesh['dp'=8,'expert'=32] {'dp'}, use_global_device_ids=true, to_apply=%region_13.14 | all-reduce | flops 1025 | bytes 8200 | tf_op jit(solution)/shard_map/psum | solution.py:17
  856.7 60.3 %all-reduce.2 = (f32[1]{0:T(128)}, f32[1024]{0:T(1024)}) all-reduce(f32[1]{0:T(128)} %bitcast.20, f32[1024]{0:T(1024)S(1)} %get-tuple-element.12), channel_id=1, replica_groups=mesh['dp'=8,'expert'=32] {'expert'}, use_global_device_ids=true, to_apply=%region_14.15 | all-reduce | flops 1025 | bytes 8200 | tf_op jit(solution)/shard_map/psum | solution.py:17
  917.1 4.3 all-reduce.10.cloned.1.call-done
  (113 shorter events, 33.5 us)
Async XLA Ops:
  7.2 111.4 %copy-start = (bf16[1,1024,512]{2,1,0:T(8,128)(2,1)S(1)}, bf16[1,1024,512]{2,1,0:T(8,128)(2,1)}, u32[]{:S(2)}) copy-start(bf16[1,1024,512]{2,1,0:T(8,128)(2,1)} %param.14) | copy-start | bytes 3145732
  7.2 92.8 %all-gather.7.cloned.1.call-start = ((), (), s32[]{:S(2)}) async-start(), calls=%async_computation.10 | async-start | bytes 5308416 | tf_op jit(solution)/shard_map/all_gather | solution.py:37
  8.5 199.2 %copy-start.9 = (f32[212]{0:T(256)}, f32[212]{0:T(256)S(1)}, u32[]{:S(2)}) copy-start(f32[212]{0:T(256)S(1)} %broadcast_multiply_fusion.3) | copy-start | bytes 2548
  9.8 197.9 %copy-start.13 = (f32[212]{0:T(256)}, f32[212]{0:T(256)S(1)}, u32[]{:S(2)}) copy-start(f32[212]{0:T(256)S(1)} %add_rsqrt_fusion) | copy-start | bytes 2548
  12.8 127.0 %copy-start.19 = (s32[212,1]{0,1:T(1,128)}, s32[212,1]{0,1:T(1,128)S(1)}, u32[]{:S(2)}) copy-start(s32[212,1]{0,1:T(1,128)S(1)} %compare_select_fusion) | copy-start | bytes 2548
  39.4 158.6 %reduce-scatter.3.cloned.1.call-start = ((), (), s32[]{:S(2)}) async-start(), calls=%async_computation.6 | async-start | bytes 5308416 | tf_op jit(solution)/shard_map/reduce_scatter | solution.py:44
  118.6 16.3 %copy-start.22 = (bf16[1,512,1024]{2,1,0:T(8,128)(2,1)S(1)}, bf16[1,512,1024]{2,1,0:T(8,128)(2,1)}, u32[]{:S(2)}) copy-start(bf16[1,512,1024]{2,1,0:T(8,128)(2,1)} %param.15) | copy-start | bytes 3145732
  139.0 68.7 %copy-start.1 = (bf16[1,212,1024]{2,1,0:T(8,128)(2,1)S(1)}, bf16[1,212,1024]{2,1,0:T(8,128)(2,1)}, u32[]{:S(2)}) copy-start(bf16[1,212,1024]{2,1,0:T(8,128)(2,1)} %param.9) | copy-start | bytes 1302532
  139.0 68.7 %copy-start.7 = (f32[1024]{0:T(1024)S(1)}, f32[1024]{0:T(1024)}, u32[]{:S(2)}) copy-start(f32[1024]{0:T(1024)} %param.12) | copy-start | bytes 12292
  139.0 69.0 %copy-start.5 = (f32[1024,32]{0,1:T(8,128)S(1)}, f32[1024,32]{0,1:T(8,128)}, u32[]{:S(2)}) copy-start(f32[1024,32]{0,1:T(8,128)} %param.13) | copy-start | bytes 393220
  139.0 69.0 %copy-start.11 = (s32[1,212,1]{1,2,0:T(1,128)S(1)}, s32[1,212,1]{1,2,0:T(1,128)}, u32[]{:S(2)}) copy-start(s32[1,212,1]{1,2,0:T(1,128)} %param.10) | copy-start | bytes 2548
  139.8 85.0 %copy-start.20 = (f32[16]{0:T(128)}, f32[16]{0:T(128)S(1)}, u32[]{:S(2)}) copy-start(f32[16]{0:T(128)S(1)} %compare_convert_fusion) | copy-start | bytes 196
  139.8 83.7 %copy-start.15 = (s32[1024]{0:T(1024)}, s32[1024]{0:T(1024)S(1)}, u32[]{:S(2)}) copy-start(s32[1024]{0:T(1024)S(1)} %pad_clamp_fusion) | copy-start | bytes 12292
  200.2 23.0 %all-to-all-start.1 = ((bf16[1,32,9,1024]{3,2,0,1:T(8,128)(2,1)}), bf16[1,32,9,1024]{3,2,0,1:T(8,128)(2,1)S(1)}, u32[]{:S(2)}, u32[]{:S(2)}) async-start(bf16[1,32,9,1024]{3,2,0,1:T(8,128)(2,1)} %bitcast.148), calls=%async_computation.2 | async-start | bytes 2097152 | tf_op jit(solution)/shard_map/all_to_all | solution.py:51
  207.7 117.8 %all-gather.9.cloned.1.call-start = ((), (), s32[]{:S(2)}) async-start(), calls=%async_computation.11 | async-start | bytes 1052672 | tf_op jit(solution)/shard_map/all_gather | solution.py:109
  208.8 14.7 %copy-start.16 = (f32[212]{0:T(256)}, f32[212]{0:T(256)S(1)}, u32[]{:S(2)}) copy-start(f32[212]{0:T(256)S(1)} %fusion.16) | copy-start | bytes 2548
  208.8 15.8 %copy-start.17 = (f32[212]{0:T(256)}, f32[212]{0:T(256)S(1)}, u32[]{:S(2)}) copy-start(f32[212]{0:T(256)S(1)} %add_divide_fusion) | copy-start | bytes 2548
  224.6 5.2 copy-start.2
  226.8 359.4 %copy-start.6 = (f32[1024]{0:T(1024)S(1)}, f32[1024]{0:T(1024)}, u32[]{:S(2)}) copy-start(f32[1024]{0:T(1024)} %broadcast_divide_fusion) | copy-start | bytes 12292
  226.8 359.4 %all-reduce.12.cloned.1.call-start = ((), (), s32[]{:S(2)}) async-start(), calls=%async_computation.13 | async-start | bytes 2097152
  228.4 360.6 %copy-start.21 = (f32[16]{0:T(128)S(1)}, f32[16]{0:T(128)}, u32[]{:S(2)}) copy-start(f32[16]{0:T(128)} %copy-done.20) | copy-start | bytes 196
  228.4 360.7 %copy-start.18 = (f32[212]{0:T(256)S(1)}, f32[212]{0:T(256)}, u32[]{:S(2)}) copy-start(f32[212]{0:T(256)} %copy-done.17) | copy-start | bytes 2548
  329.6 344.0 %all-gather.11.cloned.1.call-start = ((), (), s32[]{:S(2)}) async-start(), calls=%async_computation.12 | async-start | bytes 5308416 | tf_op jit(solution)/shard_map/all_gather | solution.py:37
  616.5 130.4 %all-reduce.8.cloned.1.call-start = ((), (), s32[]{:S(2)}) async-start(), calls=%async_computation.8 | async-start | bytes 262144 | tf_op jit(solution)/shard_map/psum | solution.py:17
  620.5 187.8 %reduce-scatter.5.cloned.1.call-start = ((), (), s32[]{:S(2)}) async-start(), calls=%async_computation.7 | async-start | bytes 5308416 | tf_op jit(solution)/shard_map/reduce_scatter | solution.py:44
  699.0 1.4 copy-start.4
  704.8 216.5 %all-reduce.10.cloned.1.call-start = ((), (), s32[]{:S(2)}) async-start(), calls=%async_computation.9 | async-start | bytes 262144 | tf_op jit(solution)/shard_map/psum | solution.py:17
  810.4 23.2 %all-to-all-start.3 = ((bf16[1,32,9,1024]{3,2,0,1:T(8,128)(2,1)}), bf16[1,32,9,1024]{3,2,0,1:T(8,128)(2,1)}, u32[]{:S(2)}, u32[]{:S(2)}) async-start(bf16[1,32,9,1024]{3,2,0,1:T(8,128)(2,1)} %bitcast.30), calls=%async_computation.5 | async-start | bytes 2097152 | tf_op jit(solution)/shard_map/all_to_all | solution.py:51
  824.9 12.1 %copy-start.8 = (f32[1024]{0:T(1024)S(1)}, f32[1024]{0:T(1024)}, u32[]{:S(2)}) copy-start(f32[1024]{0:T(1024)} %param.12) | copy-start | bytes 12292
  824.9 12.1 %copy-start.10 = (f32[212]{0:T(256)S(1)}, f32[212]{0:T(256)}, u32[]{:S(2)}) copy-start(f32[212]{0:T(256)} %copy-done.9) | copy-start | bytes 2548
  824.9 12.1 %copy-start.12 = (s32[1,212,1]{1,2,0:T(1,128)S(1)}, s32[1,212,1]{1,2,0:T(1,128)}, u32[]{:S(2)}) copy-start(s32[1,212,1]{1,2,0:T(1,128)} %param.10) | copy-start | bytes 2548
  824.9 12.1 %copy-start.14 = (f32[212]{0:T(256)S(1)}, f32[212]{0:T(256)}, u32[]{:S(2)}) copy-start(f32[212]{0:T(256)} %copy-done.13) | copy-start | bytes 2548
  (2 other events, 2.2 us)
Sparse Core Ops, SparseCore 0:
  39.6 60.3 all-gather.6
  139.2 58.8 reduce-scatter.2
  226.9 98.4 all-gather.8
  331.3 254.8 all-reduce.11
  616.7 56.8 all-gather.10
  676.4 70.4 all-reduce.7
  749.5 58.7 reduce-scatter.4
  811.5 109.8 all-reduce.9
